TPU v7x, 32 devices: a whole 2x2x4 slice. The times are simulated.
32 devices in a mesh: grp: 16 (over z, x, core), seq: 1, prm: 2 (over y).
Axes of the slice: x: 2, y: 2, z: 4, core: 2. Of those that a mesh axis runs over, the one named last changes fastest.
Arguments:
- latent_before_step: bfloat16 [2, 16, 2, 64, 1536], P('prm', 'grp', None, 'seq'), may hold values from -40 to 40
- latent_after_step: bfloat16 [2, 16, 2, 64, 1536], P('prm', 'grp', None, 'seq'), may hold values from -6 to 6
- reference_step_means: bfloat16 [2, 16, 2, 64, 1536], P('prm', 'grp', None, 'seq'), may hold values from -6 to 6
- rewards: float32 [2, 16], P('prm', 'grp'), may hold values from -12 to 12
- sample_prompt_index: int32 [2, 16], P('prm', 'grp'), may hold values from 0 to 1, as said below
- stored_step_index: int32 [2, 16, 2], P('prm', 'grp'), may hold values from 1 to 9
- modulation: float32 [10, 2, 1536], replicated, may hold values from -3 to 3
- projection_weight: bfloat16 [1536, 2304], P(None, 'grp'), may hold values from -0.15625 to 0.15625
- output_weight: bfloat16 [768, 1536], P(None, 'grp'), may hold values from -0.21875 to 0.21875
- query_norm_gain: float32 [64], replicated, may hold values from 0.1 to 1.9
- key_norm_gain: float32 [64], replicated, may hold values from 0.1 to 1.9
- projection_down_weight: bfloat16 [1536, 32], replicated, may hold values from -0.15625 to 0.15625
- projection_up_weight: bfloat16 [32, 2304], replicated, may hold values from -1 to 1
- output_down_weight: bfloat16 [768, 32], replicated, may hold values from -0.21875 to 0.21875
- output_up_weight: bfloat16 [32, 1536], replicated, may hold values from -1 to 1
Outputs:
- grad_a_qkv: float32 [1536, 32], P('grp')
- projection_up_gradient: float32 [32, 2304], P(None, 'grp')
- grad_a_out: float32 [768, 32], P('grp')
- output_up_gradient: float32 [32, 1536], P(None, 'grp')
Inputs may be any that keep to these rules, and one draw needn't show every extreme that they name: `sample_prompt_index`: in each row each of 0 and 1 stands exactly 8 times.
All inputs are finite; a program needn't handle non-finite values.
Results may differ from a plain program's by a relative error of at most 0.014.
Values may be sent and summed in bfloat16 or wider, within the bound.
A program may use at most 64 MiB of HBM per device.

v0:
```python
import jax
import jax.numpy as jnp
from jax import lax
from jax.sharding import PartitionSpec as P

SCHED = 10


ETA = 0.7
BETA = 0.1
ADAPTER_SCALE = 2.0


def rms_forward(values, gain_vec):
    inverse = lax.rsqrt(jnp.mean(values * values, axis=-1, keepdims=True) + 1e-06)
    return (values * inverse * gain_vec, inverse)


def rms_backward(values, inverse, gain_vec, upstream):
    scaled = upstream * gain_vec
    return inverse * scaled - values * inverse**3 * jnp.mean(
        scaled * values, axis=-1, keepdims=True
    )


def per_device(
    latent_before_step,
    latent_after_step,
    reference_step_means,
    rewards,
    sample_prompt_index,
    stored_step_index,
    modulation,
    projection_weight,
    output_weight,
    query_norm_gain,
    key_norm_gain,
    projection_down_weight,
    projection_up_weight,
    output_down_weight,
    output_up_weight,
):
    steps_here = latent_before_step.shape[2]
    local_tokens = latent_before_step.shape[3]
    model_width = latent_before_step.shape[4]
    head_size = query_norm_gain.shape[0]
    inner_width = output_weight.shape[0]
    head_count = inner_width // head_size
    grp_count = lax.axis_size("grp")
    row_count = steps_here * local_tokens
    score_scale = head_size ** (-0.5)
    step_size = 1.0 / SCHED
    sample_number = lax.axis_size("prm") * grp_count * steps_here
    member = (sample_prompt_index[0, 0] == jnp.arange(2, dtype=jnp.int32)).astype(jnp.float32)
    reward = rewards[0, 0]
    totals = lax.psum(member * reward, "grp")
    advantage_values = reward - jnp.sum(member * totals) / (grp_count // 2)
    full_qkv, full_out = (
        lax.all_gather(projection_weight, "grp", axis=1, tiled=True),
        lax.all_gather(output_weight, "grp", axis=1, tiled=True),
    )
    timestep_values = stored_step_index[0, 0]
    time_now = 1.0 - timestep_values.astype(jnp.float32) / SCHED
    variance = ETA * ETA * time_now / (1.0 - time_now) / SCHED
    coupling = ETA * ETA / (2.0 * (1.0 - time_now))
    mod_rows = jnp.take(modulation, timestep_values, axis=0)
    shift_rows = mod_rows[:, 0][:, None, :]
    scale_rows = mod_rows[:, 1][:, None, :]
    state_now = latent_before_step[0, 0].astype(jnp.float32)
    centre = jnp.mean(state_now, axis=-1, keepdims=True)
    spread = jnp.mean((state_now - centre) ** 2, axis=-1, keepdims=True)
    normed = (state_now - centre) * lax.rsqrt(spread + 1e-06)
    input_rows = (
        (normed * (1.0 + scale_rows) + shift_rows)
        .astype(jnp.bfloat16)
        .reshape(row_count, model_width)
    )
    projection_lowrank = jnp.dot(
        input_rows, projection_down_weight, preferred_element_type=jnp.float32
    ).astype(jnp.bfloat16)
    projected_rows = jnp.dot(
        input_rows, full_qkv, preferred_element_type=jnp.float32
    ) + ADAPTER_SCALE * jnp.dot(
        projection_lowrank, projection_up_weight, preferred_element_type=jnp.float32
    )
    projected_rows = projected_rows.reshape(steps_here, local_tokens, 3, head_count, head_size)
    query_raw = projected_rows[:, :, 0]
    key_raw = projected_rows[:, :, 1]
    value_raw = projected_rows[:, :, 2]
    query_norm, query_inverse = rms_forward(query_raw, query_norm_gain)
    key_norm, key_inverse = rms_forward(key_raw, key_norm_gain)
    query_heads = jnp.transpose(query_norm.astype(jnp.bfloat16), (0, 2, 1, 3))
    key_local = jnp.transpose(key_norm.astype(jnp.bfloat16), (0, 2, 3, 1))
    value_local = jnp.transpose(value_raw.astype(jnp.bfloat16), (0, 2, 3, 1))
    key_cols, value_cols = (
        lax.all_gather(key_local, "seq", axis=3, tiled=True),
        lax.all_gather(value_local, "seq", axis=3, tiled=True),
    )
    scores = (
        jnp.einsum("shqd,shdk->shqk", query_heads, key_cols, preferred_element_type=jnp.float32)
        * score_scale
    )
    weights = jnp.exp(scores)
    attn_probs = weights / jnp.sum(weights, axis=-1, keepdims=True)
    probs_bf = attn_probs.astype(jnp.bfloat16)
    attended_heads = jnp.einsum(
        "shqk,shdk->shqd", probs_bf, value_cols, preferred_element_type=jnp.float32
    ).astype(jnp.bfloat16)
    attended_token_rows = jnp.transpose(attended_heads, (0, 2, 1, 3)).reshape(
        row_count, inner_width
    )
    output_lowrank = jnp.dot(
        attended_token_rows, output_down_weight, preferred_element_type=jnp.float32
    ).astype(jnp.bfloat16)
    predicted_velocity = jnp.dot(
        attended_token_rows, full_out, preferred_element_type=jnp.float32
    ) + ADAPTER_SCALE * jnp.dot(
        output_lowrank, output_up_weight, preferred_element_type=jnp.float32
    )
    predicted_velocity = predicted_velocity.reshape(steps_here, local_tokens, model_width)
    time_col = time_now[:, None, None]
    var_col = variance[:, None, None]
    coup_col = coupling[:, None, None]
    mean_now = state_now - step_size * (
        predicted_velocity + coup_col * (state_now + (1.0 - time_col) * predicted_velocity)
    )
    residual = latent_after_step[0, 0].astype(jnp.float32) - mean_now
    ref_drift = mean_now - reference_step_means[0, 0].astype(jnp.float32)
    grad_mean = (-advantage_values * residual + BETA * ref_drift) / (sample_number * var_col)
    velocity_gradient = (
        (grad_mean * (-step_size * (1.0 + coup_col * (1.0 - time_col))))
        .astype(jnp.bfloat16)
        .reshape(row_count, model_width)
    )
    output_up_gradient = ADAPTER_SCALE * jnp.dot(
        output_lowrank.T, velocity_gradient, preferred_element_type=jnp.float32
    )
    output_lowrank_gradient = (
        ADAPTER_SCALE
        * jnp.dot(velocity_gradient, output_up_weight.T, preferred_element_type=jnp.float32)
    ).astype(jnp.bfloat16)
    grad_a_out = jnp.dot(
        attended_token_rows.T, output_lowrank_gradient, preferred_element_type=jnp.float32
    )
    attended_gradient = jnp.dot(
        velocity_gradient, full_out.T, preferred_element_type=jnp.float32
    ) + jnp.dot(output_lowrank_gradient, output_down_weight.T, preferred_element_type=jnp.float32)
    grad_att_heads = jnp.transpose(
        attended_gradient.astype(jnp.bfloat16).reshape(
            steps_here, local_tokens, head_count, head_size
        ),
        (0, 2, 1, 3),
    )
    grad_probs = jnp.einsum(
        "shqd,shdk->shqk", grad_att_heads, value_cols, preferred_element_type=jnp.float32
    )
    row_delta = jnp.sum(
        grad_att_heads.astype(jnp.float32) * attended_heads.astype(jnp.float32),
        axis=-1,
        keepdims=True,
    )
    grad_scores = (attn_probs * (grad_probs - row_delta) * score_scale).astype(jnp.bfloat16)
    grad_query_heads = jnp.einsum(
        "shqk,shdk->shqd", grad_scores, key_cols, preferred_element_type=jnp.float32
    )
    grad_query = jnp.transpose(grad_query_heads, (0, 2, 1, 3))
    key_term = jnp.einsum(
        "shqk,shqd->shdk", grad_scores, query_heads, preferred_element_type=jnp.float32
    )
    value_term = jnp.einsum(
        "shqk,shqd->shdk", probs_bf, grad_att_heads, preferred_element_type=jnp.float32
    )
    key_owned, value_owned = (
        lax.psum_scatter(
            key_term.astype(jnp.bfloat16), "seq", scatter_dimension=3, tiled=True
        ).astype(jnp.float32),
        lax.psum_scatter(
            value_term.astype(jnp.bfloat16), "seq", scatter_dimension=3, tiled=True
        ).astype(jnp.float32),
    )
    grad_key = jnp.transpose(key_owned, (0, 3, 1, 2))
    grad_value = jnp.transpose(value_owned, (0, 3, 1, 2))
    grad_q_raw = rms_backward(query_raw, query_inverse, query_norm_gain, grad_query)
    grad_k_raw = rms_backward(key_raw, key_inverse, key_norm_gain, grad_key)
    projected_gradient = (
        jnp.stack([grad_q_raw, grad_k_raw, grad_value], axis=2)
        .astype(jnp.bfloat16)
        .reshape(row_count, 3 * inner_width)
    )
    projection_up_gradient = ADAPTER_SCALE * jnp.dot(
        projection_lowrank.T, projected_gradient, preferred_element_type=jnp.float32
    )
    projection_lowrank_gradient = (
        ADAPTER_SCALE
        * jnp.dot(projected_gradient, projection_up_weight.T, preferred_element_type=jnp.float32)
    ).astype(jnp.bfloat16)
    grad_a_qkv = jnp.dot(
        input_rows.T, projection_lowrank_gradient, preferred_element_type=jnp.float32
    )
    local_grads = (grad_a_qkv, projection_up_gradient, grad_a_out, output_up_gradient)
    owned = (
        lax.psum_scatter(
            local_grads[0].astype(jnp.bfloat16), "grp", scatter_dimension=0, tiled=True
        ).astype(jnp.float32),
        lax.psum_scatter(
            local_grads[1].astype(jnp.bfloat16), "grp", scatter_dimension=1, tiled=True
        ).astype(jnp.float32),
        lax.psum_scatter(
            local_grads[2].astype(jnp.bfloat16), "grp", scatter_dimension=0, tiled=True
        ).astype(jnp.float32),
        lax.psum_scatter(
            local_grads[3].astype(jnp.bfloat16), "grp", scatter_dimension=1, tiled=True
        ).astype(jnp.float32),
    )
    shares = lax.psum((owned[0], owned[1], owned[2], owned[3]), ("seq", "prm"))
    return (shares[0], shares[1], shares[2], shares[3])


def solution(mesh):
    in_specs = (
        P("prm", "grp", None, "seq", None),
        P("prm", "grp", None, "seq", None),
        P("prm", "grp", None, "seq", None),
        P("prm", "grp"),
        P("prm", "grp"),
        P("prm", "grp", None),
        P(),
        P(None, "grp"),
        P(None, "grp"),
        P(),
        P(),
        P(),
        P(),
        P(),
        P(),
    )
    out_specs = (P("grp", None), P(None, "grp"), P("grp", None), P(None, "grp"))
    return jax.shard_map(
        per_device, mesh=mesh, in_specs=in_specs, out_specs=out_specs, check_vma=False
    )
```

profile of v0, /device:TPU:0, one launch (start us, length us, event | category | flops | bytes accessed | tf_op | source)
XLA Modules:
  0.0 386.5 jit_solution(15898319466305555927)
XLA Ops:
  7.3 0.7 all-gather.3.cloned.1.call-update
  8.0 0.7 all-gather.5.cloned.1.call-update
  8.7 1.1 convert_reduce_fusion
  11.5 36.0 %psum.35 = f32[2]{0:T(128)S(1)} all-reduce(f32[2]{0:T(128)S(1)} %compare_select_fusion.3), channel_id=1, replica_groups=mesh['grp'=16,'seq'=1,'prm'=2] {'grp'}, use_global_device_ids=true, to_apply=%region_5.6 | all-reduce | flops 2 | bytes 16 | tf_op jit(solution)/shard_map/psum | solution.py:56
  47.5 0.6 fusion.68
  48.7 0.6 mul.310
  49.3 0.6 mul.307
  50.6 1.5 gather_fusion
  52.8 26.5 %all-gather.3.cloned.1.call-done = bf16[1536,2304]{0,1:T(8,128)(2,1)} async-done(((bf16[1536,144]{0,1:T(8,128)(2,1)}), bf16[1536,2304]{0,1:T(8,128)(2,1)}) %all-gather.3.cloned.1.call-update) | async-done | bytes 7077904 | tf_op jit(solution)/shard_map/all_gather | solution.py:59
  79.3 5.3 %fusion.87 = f32[128,2304]{1,0:T(8,128)S(1)} fusion(bf16[128,1536]{1,0:T(8,128)(2,1)S(1)} %fusion.37, bf16[1536,2304]{0,1:T(8,128)(2,1)} %all-gather.3.cloned.1.call-done), kind=kOutput, calls=%fused_computation.138 | convolution fusion | flops 905969664 | bytes 8650752 | tf_op jit(solution)/shard_map/dot_general | solution.py:81
  84.6 1.4 fusion.1
  86.0 1.8 reshape.193
  87.8 0.9 slice.27
  88.7 2.1 copy.88
  90.8 1.5 fusion.80
  92.4 1.6 copy.87
  94.6 0.6 multiply_multiply_fusion
  95.2 0.6 multiply_multiply_fusion.1
  97.1 0.8 copy-done.13
  98.7 24.0 %all-gather.5.cloned.1.call-done = bf16[768,1536]{0,1:T(8,128)(2,1)} async-done(((bf16[768,96]{0,1:T(8,128)(2,1)}), bf16[768,1536]{0,1:T(8,128)(2,1)}) %all-gather.5.cloned.1.call-update) | async-done | bytes 2359312 | tf_op jit(solution)/shard_map/all_gather | solution.py:60
  122.7 2.6 fusion.88
  125.5 0.7 fusion.44
  126.4 0.7 copy-done.1
  128.3 1.1 copy.55
  129.4 2.1 fusion.14
  131.6 1.4 fusion.50
  133.0 3.1 fusion.29
  136.1 3.1 fusion.36
  139.2 0.9 convolution_convert_fusion.4
  140.1 1.2 fusion.4
  141.3 0.7 broadcast_multiply_fusion
  142.1 0.7 broadcast_multiply_fusion.1
  142.8 0.8 copy.78
  143.9 1.0 fusion.48
  145.1 0.7 copy-done.14
  146.1 1.2 copy.61
  147.9 0.9 copy.80
  149.3 1.0 copy.74
  150.7 1.1 copy.76
  151.8 44.1 %reduce-scatter.17.cloned.1.call-done = bf16[48,32]{1,0:T(8,128)(2,1)} async-done(((bf16[768,32]{1,0:T(8,128)(2,1)}), bf16[48,32]{1,0:T(8,128)(2,1)}) %reduce-scatter.17.cloned.1.call-update) | async-done | bytes 3088
  195.9 0.8 copy.79
  196.7 57.7 %reduce-scatter.19.cloned.1.call-done = bf16[96,32]{1,0:T(8,128)(2,1)} async-done(((bf16[1536,32]{1,0:T(8,128)(2,1)}), bf16[96,32]{1,0:T(8,128)(2,1)}) %reduce-scatter.19.cloned.1.call-update) | async-done | bytes 6160
  254.3 0.8 copy.81
  255.1 57.6 %reduce-scatter.13.cloned.1.call-done = bf16[96,32]{1,0:T(8,128)(2,1)} async-done(((bf16[1536,32]{1,0:T(8,128)(2,1)}), bf16[96,32]{1,0:T(8,128)(2,1)}) %reduce-scatter.13.cloned.1.call-update) | async-done | bytes 6160
  312.7 0.8 copy.75
  313.5 55.7 %reduce-scatter.15.cloned.1.call-done = bf16[144,32]{1,0:T(8,128)(2,1)} async-done(((bf16[2304,32]{1,0:T(8,128)(2,1)}), bf16[144,32]{1,0:T(8,128)(2,1)}) %reduce-scatter.15.cloned.1.call-update) | async-done | bytes 9232
  369.2 0.8 copy.77
  370.0 9.6 %all-reduce = (f32[96,32]{0,1:T(8,128)}, f32[32,144]{1,0:T(8,128)}, f32[48,32]{0,1:T(8,128)}, f32[32,96]{1,0:T(8,128)}) all-reduce(bf16[96,32]{0,1:T(8,128)(2,1)S(1)} %copy.75, bf16[32,144]{1,0:T(8,128)(2,1)S(1)} %copy.77, bf16[48,32]{0,1:T(8,128)(2,1)S(1)} %copy.79, ...), channel_id=1, replica_groups=mesh['grp'=16,'seq'=1,'prm'=2] {'seq','prm'}, use_global_device_ids=true, to_apply=%region_11.12 | all-reduce | flops 12288 | bytes 73728 | tf_op jit(solution)/shard_map/psum | solution.py:215
  (107 shorter events, 7.8 us)
Async XLA Ops:
  7.2 77.5 %copy-start = (bf16[32,2304]{1,0:T(8,128)(2,1)S(1)}, bf16[32,2304]{1,0:T(8,128)(2,1)}, u32[]{:S(2)}) copy-start(bf16[32,2304]{1,0:T(8,128)(2,1)} %param.27) | copy-start | bytes 442372
  7.2 2.7 copy-start.6
  7.2 3.0 copy-start.26
  7.2 45.3 %copy-start.17 = (bf16[1536,32]{0,1:T(8,128)(2,1)S(1)}, bf16[1536,32]{0,1:T(8,128)(2,1)}, u32[]{:S(2)}) copy-start(bf16[1536,32]{0,1:T(8,128)(2,1)} %param.26) | copy-start | bytes 294916
  7.2 72.1 %all-gather.3.cloned.1.call-start = ((), (), s32[]{:S(2)}) async-start(), calls=%async_computation.4 | async-start | bytes 7520256 | tf_op jit(solution)/shard_map/all_gather | solution.py:59
  7.9 114.8 %all-gather.5.cloned.1.call-start = ((), (), s32[]{:S(2)}) async-start(), calls=%async_computation.5 | async-start | bytes 2506752 | tf_op jit(solution)/shard_map/all_gather | solution.py:60
  8.7 187.2 %reduce-scatter.17.cloned.1.call-start = ((), (), s32[]{:S(2)}) async-start(), calls=%async_computation.8 | async-start | bytes 208896
  52.5 32.1 %copy-start.2 = (bf16[128,1536]{1,0:T(8,128)(2,1)}, bf16[128,1536]{1,0:T(8,128)(2,1)S(1)}, u32[]{:S(2)}) copy-start(bf16[128,1536]{1,0:T(8,128)(2,1)S(1)} %fusion.37) | copy-start | bytes 1179652
  52.8 31.9 %copy-start.19 = (bf16[128,32]{0,1:T(8,128)(2,1)}, bf16[128,32]{0,1:T(8,128)(2,1)S(1)}, u32[]{:S(2)}) copy-start(bf16[128,32]{0,1:T(8,128)(2,1)S(1)} %convolution_convert_fusion.6) | copy-start | bytes 24580
  92.3 1.6 copy-start.4
  94.4 1.5 copy-start.24
  94.4 1.5 copy-start.25
  95.2 40.8 %copy-start.16 = (f32[2,64,12]{1,2,0:T(8,128)}, f32[2,64,12]{1,2,0:T(8,128)S(1)}, u32[]{:S(2)}) copy-start(f32[2,64,12]{1,2,0:T(8,128)S(1)} %get-tuple-element.17) | copy-start | bytes 18436
  95.8 1.0 copy-start.8
  96.8 1.6 copy-start.15
  97.1 0.8 copy-start.13
  98.6 26.7 %copy-start.23 = (bf16[128,32]{0,1:T(8,128)(2,1)}, bf16[128,32]{0,1:T(8,128)(2,1)S(1)}, u32[]{:S(2)}) copy-start(bf16[128,32]{0,1:T(8,128)(2,1)S(1)} %convolution_convert_fusion.5) | copy-start | bytes 24580
  98.7 26.7 %copy-start.7 = (bf16[1,1,2,64,1536]{4,3,2,1,0:T(8,128)(2,1)S(1)}, bf16[1,1,2,64,1536]{4,3,2,1,0:T(8,128)(2,1)}, u32[]{:S(2)}) copy-start(bf16[1,1,2,64,1536]{4,3,2,1,0:T(8,128)(2,1)} %param.15) | copy-start | bytes 1179652
  98.7 26.7 %copy-start.18 = (bf16[32,1536]{1,0:T(8,128)(2,1)S(1)}, bf16[32,1536]{1,0:T(8,128)(2,1)}, u32[]{:S(2)}) copy-start(bf16[32,1536]{1,0:T(8,128)(2,1)} %param.29) | copy-start | bytes 294916
  98.7 26.7 %copy-start.29 = (f32[128]{0:T(128)S(1)}, f32[128]{0:T(128)}, u32[]{:S(2)}) copy-start(f32[128]{0:T(128)} %mul.310) | copy-start | bytes 1540
  98.7 26.7 %copy-start.30 = (f32[128]{0:T(128)S(1)}, f32[128]{0:T(128)}, u32[]{:S(2)}) copy-start(f32[128]{0:T(128)} %mul.307) | copy-start | bytes 1540
  122.7 2.7 copy-start.27
  122.7 2.7 copy-start.28
  125.5 1.7 copy-start.1
  126.2 1.4 copy-start.10
  127.1 0.6 copy-start.21
  128.3 3.3 copy-start.5
  129.4 2.1 copy-start.9
  139.2 4.7 %copy-start.12 = (f32[2,64,12,64]{1,3,2,0:T(8,128)S(1)}, f32[2,64,12,64]{1,3,2,0:T(8,128)}, u32[]{:S(2)}) copy-start(f32[2,64,12,64]{1,3,2,0:T(8,128)} %get-tuple-element.21) | copy-start | bytes 1179652
  142.8 2.1 copy-start.11
  142.8 2.1 copy-start.22
  143.6 110.7 %reduce-scatter.19.cloned.1.call-start = ((), (), s32[]{:S(2)}) async-start(), calls=%async_computation.9 | async-start | bytes 417792
  144.8 1.0 copy-start.14
  147.4 1.6 copy-start.3
  148.8 1.5 copy-start.20
  148.9 163.8 %reduce-scatter.13.cloned.1.call-start = ((), (), s32[]{:S(2)}) async-start(), calls=%async_computation.6 | async-start | bytes 417792
  150.3 218.9 %reduce-scatter.15.cloned.1.call-start = ((), (), s32[]{:S(2)}) async-start(), calls=%async_computation.7 | async-start | bytes 626688
Sparse Core Ops, SparseCore 0:
  10.3 68.9 all-gather.2
  81.5 41.1 all-gather.4
  143.8 52.0 reduce-scatter.16
  199.2 55.0 reduce-scatter.18
  257.7 55.0 reduce-scatter.12
  316.1 52.9 reduce-scatter.14
where the time goes:
time: 387 us; the launch traced here: 386 us
  waiting for transfers between devices  267 us (69%)
  blocking collectives  45.6 us (12%)
  local copies, waits for them, and re-layouts  25.4 us (7%)
  matrix products  24.6 us (6%)
  between operations  16.6 us (4%)
  other arithmetic  6.8 us (2%)
    unnamed x10, waiting for transfers between devices  216 us
    psum x1, blocking collectives, per_device(): totals = lax.psum(member * reward, 'grp')  36 us
    all_gather x1, waiting for transfers between devices, per_device(): lax.all_gather(projection_weight, 'grp', axis=1, tiled=True)  26.5 us
    all_gather x1, waiting for transfers between devices, per_device(): lax.all_gather(output_weight, 'grp', axis=1, tiled=True)  24 us
    unnamed x74, local copies, waits for them, and re-layouts  14.1 us
    psum x1, blocking collectives, per_device(): shares = lax.psum((owned[0], owned[1], owned[2], owned[3]), ('seq', 'prm'))  9.62 us
  transfers between devices with their start and end apart: 6, of which 6 were waited for; matrix products, arithmetic and copies ran while one was open for 9% of the time, Pallas kernels for 0%

commit v1 on v0

--- a/solution.py
+++ b/solution.py
@@ -1,6 +1,10 @@
+import functools
+
 import jax
 import jax.numpy as jnp
 from jax import lax
+from jax.experimental import pallas as pl
+from jax.experimental.pallas import tpu as pltpu
 from jax.sharding import PartitionSpec as P
 
 SCHED = 10
@@ -20,6 +24,283 @@
     scaled = upstream * gain_vec
     return inverse * scaled - values * inverse**3 * jnp.mean(
         scaled * values, axis=-1, keepdims=True
+    )
+
+
+MESH = pl.DeviceIdType.MESH
+CHIPS = 8
+PART = 64
+
+
+def ring_place(position):
+    side = position // 4
+    along = position * (1 - side) + (7 - position) * side
+    return along * 2 + side
+
+
+def enter(me, row, members):
+    barrier = pltpu.get_barrier_semaphore()
+    for offset in range(1, members):
+        pl.semaphore_signal(
+            barrier, inc=1, device_id=((me + offset) % members, 0, row), device_id_type=MESH
+        )
+    pl.semaphore_signal(barrier, inc=1, device_id=(me, 0, 1 - row), device_id_type=MESH)
+    pl.semaphore_wait(barrier, members)
+
+
+def gather_kernel(
+    own_ref,
+    note_ref,
+    full_ref,
+    notes_ref,
+    ring_send,
+    ring_recv,
+    core_send,
+    core_recv,
+    row_send,
+    row_recv,
+    row_core_send,
+    row_core_recv,
+    own_sem,
+    own_send,
+    own_recv,
+    note_send,
+    note_recv,
+    note_sem,
+):
+    me = lax.axis_index("grp")
+    row = lax.axis_index("prm")
+    core = me % 2
+    side = (me // 2) % 2
+    along = me // 4
+    place = along * (1 - side) + (7 - along) * side
+    sibling = (me - core + (1 - core), 0, row)
+    partner = (me, 0, 1 - row)
+    enter(me, row, 2 * CHIPS)
+
+    def index_of(position):
+        return ring_place((position + 2 * CHIPS) % CHIPS) * 2 + core
+
+    def rows_of(part, of_row):
+        start = 0 if part == 0 else pl.multiple_of(PART * (1 + of_row), PART)
+        return pl.ds(start, PART)
+
+    def remote(src, dst, send, recv, target):
+        return pltpu.make_async_remote_copy(
+            src_ref=src,
+            dst_ref=dst,
+            send_sem=send,
+            recv_sem=recv,
+            device_id=target,
+            device_id_type=MESH,
+        )
+
+    def ring_copy(way, step, part):
+        sign = 1 - 2 * way
+        block = index_of(place - sign * step)
+        rows = rows_of(part, row)
+        src = own_ref.at[rows] if step == 0 else full_ref.at[block, rows]
+        return remote(
+            src,
+            full_ref.at[block, rows],
+            ring_send.at[way, step, part],
+            ring_recv.at[way, step, part],
+            (index_of(place + sign), 0, row),
+        )
+
+    def arrived(way, step):
+        return index_of(place - (1 - 2 * way) * (step + 1))
+
+    def valid(way, step, part):
+        return step < 3 or (step == 3 and way == part)
+
+    sends = []
+    for part in range(2):
+        for way in range(2):
+            copy = ring_copy(way, 0, part)
+            copy.start()
+            sends.append(copy)
+    notes = []
+    for offset in range(1, 2 * CHIPS):
+        copy = remote(
+            note_ref,
+            notes_ref.at[me],
+            note_send.at[offset],
+            note_recv.at[offset],
+            ((me + offset) % (2 * CHIPS), 0, row),
+        )
+        copy.start()
+        notes.append(copy)
+    own_core = remote(own_ref, full_ref.at[me], own_send, own_recv, sibling)
+    own_core.start()
+    own_copy = pltpu.make_async_copy(own_ref, full_ref.at[me], own_sem)
+    own_copy.start()
+    note_copy = pltpu.make_async_copy(note_ref, notes_ref.at[me], note_sem)
+    note_copy.start()
+
+    relays = []
+    rows_over = {}
+
+    def row_arrivals(step):
+        for way in range(2):
+            if not valid(way, step, 1):
+                continue
+            rows_over[way, step].wait_recv()
+            block = full_ref.at[arrived(way, step), rows_of(1, 1 - row)]
+            copy = remote(
+                block, block, row_core_send.at[way, step], row_core_recv.at[way, step], sibling
+            )
+            copy.start()
+            relays.append(copy)
+
+    for step in range(4):
+        for part in range(2):
+            for way in range(2):
+                if not valid(way, step, part):
+                    continue
+                ring_copy(way, step, part).wait_recv()
+                if valid(way, step + 1, part):
+                    copy = ring_copy(way, step + 1, part)
+                    copy.start()
+                    sends.append(copy)
+                block = full_ref.at[arrived(way, step), rows_of(part, row)]
+                if part == 1:
+                    copy = remote(
+                        block, block, row_send.at[way, step], row_recv.at[way, step], partner
+                    )
+                    copy.start()
+                    rows_over[way, step] = copy
+                copy = remote(
+                    block,
+                    block,
+                    core_send.at[way, step, part],
+                    core_recv.at[way, step, part],
+                    sibling,
+                )
+                copy.start()
+                relays.append(copy)
+        if step:
+            row_arrivals(step - 1)
+    row_arrivals(3)
+
+    for copy in sends:
+        copy.wait_send()
+    for copy in rows_over.values():
+        copy.wait_send()
+    for copy in relays:
+        copy.wait()
+    for copy in notes:
+        copy.wait()
+    own_core.wait()
+    own_copy.wait()
+    note_copy.wait()
+
+
+def gather_weights(own, note):
+    members = 2 * CHIPS
+    dma = pltpu.SemaphoreType.DMA
+    return pl.pallas_call(
+        gather_kernel,
+        out_shape=(
+            jax.ShapeDtypeStruct((members,) + own.shape, own.dtype),
+            jax.ShapeDtypeStruct((members,) + note.shape, note.dtype),
+        ),
+        in_specs=[pl.BlockSpec(memory_space=pltpu.VMEM)] * 2,
+        out_specs=(
+            pl.BlockSpec(memory_space=pl.ANY),
+            pl.BlockSpec(memory_space=pltpu.VMEM),
+        ),
+        scratch_shapes=[
+            dma((2, 4, 2)),
+            dma((2, 4, 2)),
+            dma((2, 4, 2)),
+            dma((2, 4, 2)),
+            dma((2, 4)),
+            dma((2, 4)),
+            dma((2, 4)),
+            dma((2, 4)),
+            dma,
+            dma,
+            dma,
+            dma((members,)),
+            dma((members,)),
+            dma,
+        ],
+        compiler_params=pltpu.CompilerParams(collective_id=0, has_side_effects=True),
+        name="gather_weights",
+    )(own, note)
+
+
+def reduce_kernel(
+    parts_ref, out_ref, landed, total, other, send_sem, recv_sem, row_send, row_recv
+):
+    me = lax.axis_index("grp")
+    row = lax.axis_index("prm")
+    members = parts_ref.shape[0]
+    enter(me, row, members)
+    copies = []
+    for offset in range(1, members):
+        target = (me + offset) % members
+        copy = pltpu.make_async_remote_copy(
+            src_ref=parts_ref.at[target],
+            dst_ref=landed.at[offset],
+            send_sem=send_sem.at[offset],
+            recv_sem=recv_sem.at[offset],
+            device_id=(target, 0, row),
+            device_id_type=MESH,
+        )
+        copy.start()
+        copies.append(copy)
+    running = parts_ref[me].astype(jnp.float32)
+    for offset in range(1, members):
+        copies[offset - 1].wait_recv()
+        running = running + landed[offset].astype(jnp.float32)
+    total[...] = running
+    swap = pltpu.make_async_remote_copy(
+        src_ref=total,
+        dst_ref=other,
+        send_sem=row_send,
+        recv_sem=row_recv,
+        device_id=(me, 0, 1 - row),
+        device_id_type=MESH,
+    )
+    swap.start()
+    for copy in copies:
+        copy.wait_send()
+    swap.wait()
+    out_ref[...] = total[...] + other[...]
+
+
+def reduce_shares(parts):
+    members = parts.shape[0]
+    share = parts.shape[1:]
+    dma = pltpu.SemaphoreType.DMA
+    return pl.pallas_call(
+        reduce_kernel,
+        out_shape=jax.ShapeDtypeStruct(share, jnp.float32),
+        in_specs=[pl.BlockSpec(memory_space=pltpu.VMEM)],
+        out_specs=pl.BlockSpec(memory_space=pltpu.VMEM),
+        scratch_shapes=[
+            pltpu.VMEM(parts.shape, parts.dtype),
+            pltpu.VMEM(share, jnp.float32),
+            pltpu.VMEM(share, jnp.float32),
+            dma((members,)),
+            dma((members,)),
+            dma,
+            dma,
+        ],
+        compiler_params=pltpu.CompilerParams(collective_id=1, has_side_effects=True),
+        name="reduce_shares",
+    )(parts)
+
+
+def direct_fits(projection_weight, output_weight):
+    return (
+        lax.axis_size("grp") == 2 * CHIPS
+        and lax.axis_size("seq") == 1
+        and lax.axis_size("prm") == 2
+        and projection_weight.shape[1] + output_weight.shape[1] // 2 == 3 * PART
+        and projection_weight.shape[0] == 2 * output_weight.shape[0]
     )
 
 
@@ -53,12 +334,34 @@
     sample_number = lax.axis_size("prm") * grp_count * steps_here
     member = (sample_prompt_index[0, 0] == jnp.arange(2, dtype=jnp.int32)).astype(jnp.float32)
     reward = rewards[0, 0]
-    totals = lax.psum(member * reward, "grp")
+    direct = direct_fits(projection_weight, output_weight)
+    if direct:
+        half = output_weight.shape[1] // 2
+        qkv_own = projection_weight.shape[1]
+        own_out = output_weight.T
+        own = jnp.concatenate(
+            [projection_weight.T, jnp.concatenate([own_out[:half], own_out[half:]], axis=1)],
+            axis=0,
+        )
+        note = jnp.broadcast_to(
+            jnp.pad(member * reward, (0, 6))[:, None], (8, 128)
+        )
+        full, notes = gather_weights(own, note)
+        totals = jnp.sum(notes[:, :2, 0], axis=0)
+        full_qkv = full[:, :qkv_own].reshape(-1, model_width)
+        full_out = (
+            full[:, qkv_own:]
+            .reshape(grp_count, half, 2, inner_width)
+            .transpose(0, 2, 1, 3)
+            .reshape(model_width, inner_width)
+        )
+    else:
+        totals = lax.psum(member * reward, "grp")
+        full_qkv, full_out = (
+            lax.all_gather(projection_weight.T, "grp", axis=0, tiled=True),
+            lax.all_gather(output_weight.T, "grp", axis=0, tiled=True),
+        )
     advantage_values = reward - jnp.sum(member * totals) / (grp_count // 2)
-    full_qkv, full_out = (
-        lax.all_gather(projection_weight, "grp", axis=1, tiled=True),
-        lax.all_gather(output_weight, "grp", axis=1, tiled=True),
-    )
     timestep_values = stored_step_index[0, 0]
     time_now = 1.0 - timestep_values.astype(jnp.float32) / SCHED
     variance = ETA * ETA * time_now / (1.0 - time_now) / SCHED
@@ -78,8 +381,8 @@
     projection_lowrank = jnp.dot(
         input_rows, projection_down_weight, preferred_element_type=jnp.float32
     ).astype(jnp.bfloat16)
-    projected_rows = jnp.dot(
-        input_rows, full_qkv, preferred_element_type=jnp.float32
+    projected_rows = jnp.einsum(
+        "rk,ck->rc", input_rows, full_qkv, preferred_element_type=jnp.float32
     ) + ADAPTER_SCALE * jnp.dot(
         projection_lowrank, projection_up_weight, preferred_element_type=jnp.float32
     )
@@ -112,8 +415,8 @@
     output_lowrank = jnp.dot(
         attended_token_rows, output_down_weight, preferred_element_type=jnp.float32
     ).astype(jnp.bfloat16)
-    predicted_velocity = jnp.dot(
-        attended_token_rows, full_out, preferred_element_type=jnp.float32
+    predicted_velocity = jnp.einsum(
+        "rk,ck->rc", attended_token_rows, full_out, preferred_element_type=jnp.float32
     ) + ADAPTER_SCALE * jnp.dot(
         output_lowrank, output_up_weight, preferred_element_type=jnp.float32
     )
@@ -143,7 +446,7 @@
         attended_token_rows.T, output_lowrank_gradient, preferred_element_type=jnp.float32
     )
     attended_gradient = jnp.dot(
-        velocity_gradient, full_out.T, preferred_element_type=jnp.float32
+        velocity_gradient, full_out, preferred_element_type=jnp.float32
     ) + jnp.dot(output_lowrank_gradient, output_down_weight.T, preferred_element_type=jnp.float32)
     grad_att_heads = jnp.transpose(
         attended_gradient.astype(jnp.bfloat16).reshape(
@@ -198,22 +501,30 @@
         input_rows.T, projection_lowrank_gradient, preferred_element_type=jnp.float32
     )
     local_grads = (grad_a_qkv, projection_up_gradient, grad_a_out, output_up_gradient)
-    owned = (
-        lax.psum_scatter(
-            local_grads[0].astype(jnp.bfloat16), "grp", scatter_dimension=0, tiled=True
-        ).astype(jnp.float32),
-        lax.psum_scatter(
-            local_grads[1].astype(jnp.bfloat16), "grp", scatter_dimension=1, tiled=True
-        ).astype(jnp.float32),
-        lax.psum_scatter(
-            local_grads[2].astype(jnp.bfloat16), "grp", scatter_dimension=0, tiled=True
-        ).astype(jnp.float32),
-        lax.psum_scatter(
-            local_grads[3].astype(jnp.bfloat16), "grp", scatter_dimension=1, tiled=True
-        ).astype(jnp.float32),
-    )
-    shares = lax.psum((owned[0], owned[1], owned[2], owned[3]), ("seq", "prm"))
-    return (shares[0], shares[1], shares[2], shares[3])
+    rank = projection_lowrank.shape[1]
+    wide = (local_grads[0].T, local_grads[1], local_grads[2].T, local_grads[3])
+    widths = [grad.shape[1] // grp_count for grad in wide]
+    packed = jnp.concatenate(
+        [
+            grad.astype(jnp.bfloat16).reshape(rank, grp_count, width)
+            for grad, width in zip(wide, widths)
+        ],
+        axis=2,
+    )
+    if direct:
+        share = reduce_shares(packed.transpose(1, 0, 2))
+    else:
+        share = lax.psum_scatter(
+            packed, "grp", scatter_dimension=1, tiled=True
+        ).astype(jnp.float32).reshape(rank, -1)
+        share = lax.psum(share, ("seq", "prm"))
+    first, second, third = widths[0], widths[0] + widths[1], sum(widths[:3])
+    return (
+        share[:, :first].T,
+        share[:, first:second],
+        share[:, second:third].T,
+        share[:, third:],
+    )
 
 
 def solution(mesh):

time: 387 us -> 147 us (0.38)
  waiting for transfers between devices: 267 us -> 0 us
  Pallas kernels: 0 us -> 67.9 us
  blocking collectives: 45.6 us -> 0 us
  local copies, waits for them, and re-layouts: 25.4 us -> 39.8 us
  between operations: 16.6 us -> 3.18 us
  other arithmetic: 6.8 us -> 15.5 us
  matrix products: 24.6 us -> 18.9 us
    unnamed x10 -> x0, waiting for transfers between devices: 216 us -> none
    pallas_call x0 -> x2, Pallas kernels: none -> 67.9 us  [the longest x1 52.9 us: gather_weights(): pl.pallas_call(gather_kernel, out_shape=(jax.ShapeDtypeStruct((members,)...]
    all_gather x2 -> x0, waiting for transfers between devices: 50.5 us -> none  [the longest x1 26.5 us: per_device(): lax.all_gather(projection_weight, 'grp', axis=1, tiled=True)]
    psum x2 -> x0, blocking collectives: 45.6 us -> none  [the longest x1 36 us: per_device(): totals = lax.psum(member * reward, 'grp')]
    slice x0 -> x5, local copies, waits for them, and re-layouts: none -> 8.26 us  [the longest x1 3.52 us: per_device(): full_qkv = full[:, :qkv_own].reshape(-1, model_width)]
    unnamed x74 -> x72, local copies, waits for them, and re-layouts: 14.1 us -> 6.11 us
  transfers between devices with their start and end apart: 6 -> 0, of which waited for: 6 -> 0; matrix products, arithmetic and copies ran while one was open for 9% -> 0% of each run, Pallas kernels for 0% -> 0%
where the time goes in v1:
time: 147 us; the launch traced here: 145 us
  Pallas kernels  67.9 us (46%)
  local copies, waits for them, and re-layouts  39.8 us (27%)
  matrix products  18.9 us (13%)
  other arithmetic  15.5 us (11%)
  between operations  3.18 us (2%)
    pallas_call x1, Pallas kernels, gather_weights(): pl.pallas_call(gather_kernel, out_shape=(jax.ShapeDtypeStruct((members,)...  52.9 us
    pallas_call x1, Pallas kernels, reduce_shares(): pl.pallas_call(reduce_kernel, out_shape=jax.ShapeDtypeStruct(share, jnp.f...  15.1 us
    unnamed x72, local copies, waits for them, and re-layouts  6.11 us
    another operation x3, other arithmetic, per_device(): jnp.stack([grad_q_raw, grad_k_raw, grad_value], axis=2).astype(jnp.bfloat16)  3.79 us
    slice x1, local copies, waits for them, and re-layouts, per_device(): full_qkv = full[:, :qkv_own].reshape(-1, model_width)  3.52 us
    reshape x2, local copies, waits for them, and re-layouts, per_device(): attended_gradient.astype(jnp.bfloat16)  3.26 us
    dot_general x1, matrix products, per_device(): jnp.einsum('shqk,shdk->shqd', grad_scores, key_cols, preferred_element_ty...  3.09 us

profile of v1, /device:TPU:0, one launch (start us, length us, event | category | flops | bytes accessed | tf_op | source)
XLA Modules:
  0.0 145.4 jit_solution(7558834388342568742)
XLA Ops:
  0.7 0.7 fusion.74
  1.4 1.5 %gather_fusion = f32[2,2,1536]{2,1,0:T(2,128)S(1)} fusion(f32[10,2,1536]{2,1,0:T(2,128)} %param.21, s32[1024]{0:T(1024)S(1)} %pad_clamp_fusion), kind=kCustom, calls=%fused_computation | custom fusion | bytes 49160 | tf_op jit(solution)/shard_map/jit(_take)/gather | solution.py:369
  2.9 0.7 compare_and_fusion
  3.7 1.1 convert_reduce_fusion
  4.9 1.3 fusion.41
  6.5 0.9 maximum_maximum_fusion.own_ref
  8.7 0.7 broadcast_in_dim.14.note_ref
  9.3 52.9 %gather_weights.1 = (bf16[16,192,1536]{2,1,0:T(8,128)(2,1)}, f32[16,8,128]{2,1,0:T(8,128)}) custom-call(bf16[192,1536]{1,0:T(8,128)(2,1)} %maximum_maximum_fusion.own_ref, f32[8,128]{1,0:T(8,128)} %broadcast_in_dim.14.note_ref), custom_call_target="tpu_custom_call" | custom-call | tf_op jit(solution)/shard_map/gather_weights/pallas_call | solution.py:202
  62.2 3.5 %slice.47 = bf16[16,144,1536]{2,1,0:T(8,128)(2,1)S(1)} slice(bf16[16,192,1536]{2,1,0:T(8,128)(2,1)} %get-tuple-element.6), slice={[0:16], [0:144], [0:1536]} | slice | bytes 14155776 | tf_op jit(solution)/shard_map/slice | solution.py:351
  65.7 2.3 %fusion.94 = f32[128,2304]{1,0:T(8,128)S(1)} fusion(bf16[128,1536]{1,0:T(8,128)(2,1)S(1)} %bitcast.235, bf16[2304,1536]{1,0:T(8,128)(2,1)S(1)} %bitcast.229), kind=kOutput, calls=%fused_computation.151 | convolution fusion | flops 905969664 | bytes 8650752 | tf_op jit(solution)/shard_map/rk,ck->rc/dot_general | solution.py:384
  69.9 1.4 fusion.1
  71.3 2.0 %reshape.277 = f32[2,64,3,12,64]{4,3,2,1,0:T(8,128)S(1)} reshape(f32[128,2304]{1,0:T(8,128)} %fusion.1) | data formatting | bytes 2359296 | tf_op jit(solution)/shard_map/reshape | solution.py:389
  73.3 1.7 %fusion.85 = (f32[2,64,1,12,64]{4,3,2,1,0:T(8,128)}, f32[2,64,1,12,64]{4,3,2,1,0:T(8,128)}) fusion(f32[2,64,3,12,64]{4,3,2,1,0:T(8,128)S(1)} %reshape.277), kind=kLoop, calls=%fused_computation.148 | loop fusion | bytes 1572864 | tf_op jit(solution)/shard_map/slice | solution.py:391
  75.0 0.7 copy-done.5
  75.7 1.6 %copy.67 = f32[2,64,1,12,64]{1,4,3,0,2:T(8,128)S(1)} copy(f32[2,64,1,12,64]{4,3,2,1,0:T(8,128)} %get-tuple-element.11) | data formatting | bytes 786432
  77.4 0.8 multiply_multiply_fusion.1
  78.7 0.6 multiply_multiply_fusion
  79.8 1.6 %slice.65 = bf16[2,64,1,12,64]{4,3,2,1,0:T(8,128)(2,1)S(1)} slice(f32[2,64,3,12,64]{4,3,2,1,0:T(8,128)} %copy-done.5), slice={[0:2], [0:64], [2:3], [0:12], [0:64]} | slice | bytes 393216 | tf_op jit(solution)/shard_map/slice | solution.py:392
  82.7 1.8 %slice.52 = bf16[16,48,1536]{2,1,0:T(8,128)(2,1)S(1)} slice(bf16[16,192,1536]{2,1,0:T(8,128)(2,1)} %get-tuple-element.6), slice={[0:16], [144:192], [0:1536]} | slice | bytes 4718592 | tf_op jit(solution)/shard_map/slice | solution.py:353
  84.8 1.8 %fusion.95 = f32[128,1536]{1,0:T(8,128)} fusion(bf16[128,768]{0,1:T(8,128)(2,1)S(1)} %reshape.257, bf16[1536,768]{1,0:T(8,128)(2,1)S(1)} %bitcast.230), kind=kOutput, calls=%fused_computation.152 | convolution fusion | flops 301989888 | bytes 3342336 | tf_op jit(solution)/shard_map/rk,ck->rc/dot_general | solution.py:418
  86.5 0.8 convolution_convert_fusion.5
  87.3 1.0 slice_reduce_fusion
  88.3 0.7 fusion.73
  89.6 1.3 add_multiply_fusion
  90.9 0.6 div.76
  91.5 1.3 div.77
  92.8 1.2 mul.329
  94.1 1.3 mul.330
  95.4 1.2 mul.332
  96.6 1.2 mul.333
  97.8 1.3 mul.345
  99.1 1.4 mul.346
  100.5 2.2 %fusion.49 = bf16[128,1536]{1,0:T(8,128)(2,1)S(1)} fusion(bf16[128,1536]{1,0:T(8,128)(2,1)} %bitcast.238, f32[128,1536]{1,0:T(8,128)} %fusion.95, bf16[128,32]{0,1:T(8,128)(2,1)} %convolution_convert_fusion.5, bf16[32,1536]{1,0:T(8,128)(2,1)} %param.29, bf16[1,1,2,64,1536]{4,3,2,1,0:T(8,128)(2,1)} %param.15, bf16[128,1536]{1,0:T(8,128)(2,1)} %bitcast.239, ...), kind=kOutput, calls=%fused_computation.86 | convolution fusion | flops 16318464 | bytes 2467844 | tf_op jit(solution)/shard_map/dot_general | solution.py:420
  104.2 1.1 reshape.276
  105.3 1.6 %fusion.55 = f32[2,12,64,64]{2,3,1,0:T(8,128)S(1)} fusion(bf16[2,12,64,64]{3,1,2,0:T(8,128)(2,1)} %bitcast.233, bf16[2,64,1,12,64]{1,4,3,0,2:T(8,128)(2,1)} %copy-done.12), kind=kOutput, calls=%fused_computation.94 | convolution fusion | flops 12582912 | bytes 786432 | tf_op jit(solution)/shard_map/shqd,shdk->shqk/dot_general | solution.py:457
  107.0 2.1 %copy.40 = bf16[2,64,12,64]{1,3,2,0:T(8,128)(2,1)} copy(bf16[2,64,12,64]{3,2,1,0:T(8,128)(2,1)} %reshape.276) | data formatting | bytes 393216 | tf_op jit(solution)/shard_map/reshape | solution.py:452
  109.2 3.1 %fusion.36 = (f32[2,64,12]{1,2,0:T(8,128)}, f32[2,64,12,64]{1,3,2,0:T(8,128)}) fusion(f32[2,64,1,12,64]{1,4,3,0,2:T(8,128)S(1)} %copy-done.2, f32[64]{0:T(128)S(1)} %copy-done.33, f32[2,12,64,64]{2,3,1,0:T(8,128)S(1)} %copy-done.4, f32[2,12,64,64]{2,3,1,0:T(8,128)S(1)} %fusion.55, bf16[2,12,64,64]{2,3,1,0:T(8,128)(2,1)} %copy-done.14, ...), kind=kOutput, calls=%fused_computation.65 | convolution fusion | flops 13860927 | bytes 2372096 | tf_op jit(solution)/shard_map/shqk,shdk->shqd/dot_general | solution.py:466
  112.3 0.7 broadcast_multiply_fusion.1
  113.0 2.1 %fusion.51 = bf16[2,64,1,12,64]{1,4,3,0,2:T(8,128)(2,1)} fusion(f32[2,64,1,12,64]{1,4,3,0,2:T(8,128)S(1)} %copy-done.2, f32[2,64,12,64]{1,3,2,0:T(8,128)} %get-tuple-element.27, f32[2,64,12]{1,2,0:T(8,128)S(1)} %broadcast_multiply_fusion.1, f32[2,64,12]{1,2,0:T(8,128)S(1)} %copy-done.28, f32[2,64,12]{1,2,0:T(8,128)S(1)} %copy-done.19), kind=kLoop, calls=%fused_computation.89 | loop fusion | flops 491520 | bytes 1001472 | tf_op jit(solution)/shard_map/stack | solution.py:489
  115.1 2.5 %fusion.29 = (f32[2,64,12]{1,2,0:T(8,128)S(1)}, f32[2,64,12,64]{1,3,2,0:T(8,128)}) fusion(f32[2,64,1,12,64]{1,4,3,0,2:T(8,128)S(1)} %copy.68, f32[64]{0:T(128)} %param.25, f32[2,12,64,64]{2,3,1,0:T(8,128)S(1)} %copy-done.4, f32[2,12,64,64]{2,3,1,0:T(8,128)S(1)} %fusion.55, bf16[2,12,64,64]{2,3,1,0:T(8,128)(2,1)} %copy-done.14, ...), kind=kOutput, calls=%fused_computation.54 | convolution fusion | flops 14057535 | bytes 2372096 | tf_op jit(solution)/shard_map/shqk,shqd->shdk/dot_general | solution.py:470
  117.6 1.4 fusion.53
  119.3 0.7 copy-done.15
  120.3 1.2 copy.46
  124.9 1.1 maximum_bitcast_fusion.parts_ref
  125.9 15.1 %reduce_shares.1 = f32[32,384]{1,0:T(8,128)} custom-call(bf16[16,32,384]{2,1,0:T(8,128)(2,1)} %maximum_bitcast_fusion.parts_ref), custom_call_target="tpu_custom_call" | custom-call | tf_op jit(solution)/shard_map/reduce_shares/pallas_call | solution.py:278
  141.0 1.4 fusion.87
  142.4 1.5 %slice.54 = f32[32,144]{1,0:T(8,128)} slice(f32[32,384]{1,0:T(8,128)} %reduce_shares.1), slice={[0:32], [96:240]} | slice | bytes 36864 | tf_op jit(solution)/shard_map/slice | solution.py:524
  143.9 1.4 slice_bitcast_fusion
  (108 shorter events, 10.2 us)
Async XLA Ops:
  0.6 69.3 %copy-start = (bf16[32,2304]{1,0:T(8,128)(2,1)S(1)}, bf16[32,2304]{1,0:T(8,128)(2,1)}, u32[]{:S(2)}) copy-start(bf16[32,2304]{1,0:T(8,128)(2,1)} %param.27) | copy-start | bytes 442372
  0.6 5.5 %copy-start.6 = (bf16[1,1,2,64,1536]{4,3,2,1,0:T(8,128)(2,1)S(1)}, bf16[1,1,2,64,1536]{4,3,2,1,0:T(8,128)(2,1)}, u32[]{:S(2)}) copy-start(bf16[1,1,2,64,1536]{4,3,2,1,0:T(8,128)(2,1)} %param.15) | copy-start | bytes 1179652
  0.7 5.8 %copy-start.20 = (bf16[768,96]{0,1:T(8,128)(2,1)S(1)}, bf16[768,96]{0,1:T(8,128)(2,1)}, u32[]{:S(2)}) copy-start(bf16[768,96]{0,1:T(8,128)(2,1)} %param.23) | copy-start | bytes 442372
  0.7 5.8 %copy-start.16 = (bf16[1536,144]{0,1:T(8,128)(2,1)S(1)}, bf16[1536,144]{0,1:T(8,128)(2,1)}, u32[]{:S(2)}) copy-start(bf16[1536,144]{0,1:T(8,128)(2,1)} %param.22) | copy-start | bytes 1327108
  65.7 2.8 %copy-start.21 = (bf16[1536,32]{0,1:T(8,128)(2,1)S(1)}, bf16[1536,32]{0,1:T(8,128)(2,1)}, u32[]{:S(2)}) copy-start(bf16[1536,32]{0,1:T(8,128)(2,1)} %param.26) | copy-start | bytes 294916
  68.6 0.8 copy-start.8
  69.3 0.6 copy-start.23
  73.3 2.4 %copy-start.5 = (f32[2,64,3,12,64]{4,3,2,1,0:T(8,128)}, f32[2,64,3,12,64]{4,3,2,1,0:T(8,128)S(1)}, u32[]{:S(2)}) copy-start(f32[2,64,3,12,64]{4,3,2,1,0:T(8,128)S(1)} %reshape.277) | copy-start | bytes 3538948
  75.7 2.5 %copy-start.7 = (f32[2,64,1,12,64]{4,3,2,1,0:T(8,128)S(1)}, f32[2,64,1,12,64]{4,3,2,1,0:T(8,128)}, u32[]{:S(2)}) copy-start(f32[2,64,1,12,64]{4,3,2,1,0:T(8,128)} %get-tuple-element.10) | copy-start | bytes 1179652
  77.3 2.0 %copy-start.1 = (f32[2,64,1,12,64]{1,4,3,0,2:T(8,128)}, f32[2,64,1,12,64]{1,4,3,0,2:T(8,128)S(1)}, u32[]{:S(2)}) copy-start(f32[2,64,1,12,64]{1,4,3,0,2:T(8,128)S(1)} %copy.67) | copy-start | bytes 1179652
  78.2 1.1 copy-start.18
  78.2 1.1 copy-start.30
  78.2 1.1 copy-start.32
  79.8 2.3 %copy-start.3 = (f32[2,12,64,64]{2,3,1,0:T(8,128)}, f32[2,12,64,64]{2,3,1,0:T(8,128)S(1)}, u32[]{:S(2)}) copy-start(f32[2,12,64,64]{2,3,1,0:T(8,128)S(1)} %fusion.65) | copy-start | bytes 1179652
  81.8 0.7 copy-start.12
  82.1 2.5 %copy-start.14 = (bf16[2,12,64,64]{2,3,1,0:T(8,128)(2,1)}, bf16[2,12,64,64]{2,3,1,0:T(8,128)(2,1)S(1)}, u32[]{:S(2)}) copy-start(bf16[2,12,64,64]{2,3,1,0:T(8,128)(2,1)S(1)} %convolution_convert_fusion.1) | copy-start | bytes 589828
  84.7 1.8 %copy-start.17 = (bf16[768,32]{0,1:T(8,128)(2,1)S(1)}, bf16[768,32]{0,1:T(8,128)(2,1)}, u32[]{:S(2)}) copy-start(bf16[768,32]{0,1:T(8,128)(2,1)} %param.28) | copy-start | bytes 147460
  102.7 0.8 copy-start.10
  102.7 1.0 copy-start.22
  103.9 1.4 copy-start.25
  105.3 3.8 %copy-start.2 = (f32[2,64,1,12,64]{1,4,3,0,2:T(8,128)S(1)}, f32[2,64,1,12,64]{1,4,3,0,2:T(8,128)}, u32[]{:S(2)}) copy-start(f32[2,64,1,12,64]{1,4,3,0,2:T(8,128)} %copy-done.1) | copy-start | bytes 1179652
  105.3 3.8 %copy-start.4 = (f32[2,12,64,64]{2,3,1,0:T(8,128)S(1)}, f32[2,12,64,64]{2,3,1,0:T(8,128)}, u32[]{:S(2)}) copy-start(f32[2,12,64,64]{2,3,1,0:T(8,128)} %copy-done.3) | copy-start | bytes 1179652
  105.3 3.8 %copy-start.31 = (f32[64]{0:T(128)S(1)}, f32[64]{0:T(128)}, u32[]{:S(2)}) copy-start(f32[64]{0:T(128)} %param.25) | copy-start | bytes 772
  105.3 3.8 %copy-start.33 = (f32[64]{0:T(128)S(1)}, f32[64]{0:T(128)}, u32[]{:S(2)}) copy-start(f32[64]{0:T(128)} %param.24) | copy-start | bytes 772
  109.1 3.8 %copy-start.19 = (f32[2,64,12]{1,2,0:T(8,128)S(1)}, f32[2,64,12]{1,2,0:T(8,128)}, u32[]{:S(2)}) copy-start(f32[2,64,12]{1,2,0:T(8,128)} %copy-done.18) | copy-start | bytes 18436
  109.2 3.8 %copy-start.28 = (f32[2,64,12]{1,2,0:T(8,128)S(1)}, f32[2,64,12]{1,2,0:T(8,128)}, u32[]{:S(2)}) copy-start(f32[2,64,12]{1,2,0:T(8,128)} %get-tuple-element.18) | copy-start | bytes 18436
  115.1 2.5 %copy-start.27 = (f32[2,64,12]{1,2,0:T(8,128)S(1)}, f32[2,64,12]{1,2,0:T(8,128)}, u32[]{:S(2)}) copy-start(f32[2,64,12]{1,2,0:T(8,128)} %get-tuple-element.20) | copy-start | bytes 18436
  117.6 1.4 copy-start.13
  119.0 1.0 copy-start.15
  121.5 1.0 copy-start.9
  122.5 0.7 copy-start.24
  122.9 1.2 copy-start.26
  123.2 1.3 copy-start.11
  123.2 1.3 copy-start.29

commit v2 on v1

--- a/solution.py
+++ b/solution.py
@@ -294,13 +294,239 @@
     )(parts)
 
 
-def direct_fits(projection_weight, output_weight):
+def direct_fits(projection_weight, output_weight, row_count):
     return (
         lax.axis_size("grp") == 2 * CHIPS
         and lax.axis_size("seq") == 1
         and lax.axis_size("prm") == 2
+        and row_count == 128
         and projection_weight.shape[1] + output_weight.shape[1] // 2 == 3 * PART
         and projection_weight.shape[0] == 2 * output_weight.shape[0]
+    )
+
+
+def mm(a, b, contract=(1, 0)):
+    return lax.dot_general(
+        a, b, (((contract[0],), (contract[1],)), ((), ())), preferred_element_type=jnp.float32
+    )
+
+
+def block_kernel(
+    step_ref,
+    coef_ref,
+    full_ref,
+    before_ref,
+    after_ref,
+    means_ref,
+    modulation_ref,
+    query_gain_ref,
+    key_gain_ref,
+    down_ref,
+    up_ref,
+    out_down_ref,
+    out_up_ref,
+    parts_ref,
+    qkv,
+    out,
+    inputs,
+    projected,
+    keep,
+    att,
+    grad_att,
+    grad_proj,
+    grad_vel,
+    qkv_sem,
+    out_sem,
+):
+    members = full_ref.shape[0]
+    steps = step_ref.shape[0]
+    rows = before_ref.shape[0]
+    tokens = rows // steps
+    head = query_gain_ref.shape[0]
+    inner = out_down_ref.shape[0]
+    heads = inner // head
+    own_qkv = qkv.shape[0] // members
+    half = out.shape[0] // members // 2
+    scale = head ** (-0.5)
+
+    copies, out_copies = [], []
+    for g in range(members):
+        copies.append(
+            pltpu.make_async_copy(
+                full_ref.at[g, pl.ds(0, own_qkv)],
+                qkv.at[pl.ds(g * own_qkv, own_qkv)],
+                qkv_sem.at[g],
+            )
+        )
+    for g in range(members):
+        for j in range(2):
+            out_copies.append(
+                pltpu.make_async_copy(
+                    full_ref.at[g, pl.ds(own_qkv, half), pl.ds(j * inner, inner)],
+                    out.at[pl.ds((2 * g + j) * half, half)],
+                    out_sem.at[2 * g + j],
+                )
+            )
+    for copy in copies + out_copies:
+        copy.start()
+
+    for s in range(steps):
+        span = slice(s * tokens, (s + 1) * tokens)
+        state = before_ref[span].astype(jnp.float32)
+        centred = state - jnp.mean(state, axis=1, keepdims=True)
+        spread = jnp.mean(centred * centred, axis=1, keepdims=True)
+        rows_mod = modulation_ref[step_ref[s]]
+        normed = centred * lax.rsqrt(spread + 1e-06)
+        inputs[span] = (normed * (1.0 + rows_mod[1:2]) + rows_mod[0:1]).astype(jnp.bfloat16)
+    low = mm(inputs[...], down_ref[...])
+    low_t = low.T.astype(jnp.bfloat16)
+    low_term = ADAPTER_SCALE * mm(up_ref[...], low_t, (0, 0))
+    for g in range(members):
+        span = slice(g * own_qkv, (g + 1) * own_qkv)
+        copies[g].wait()
+        projected[span] = mm(qkv[span], inputs[...], (1, 1)) + low_term[span]
+
+    same = (lax.broadcasted_iota(jnp.int32, (rows, rows), 0) // tokens) == (
+        lax.broadcasted_iota(jnp.int32, (rows, rows), 1) // tokens
+    )
+
+    def raw(which, h):
+        start = which * inner + h * head
+        return projected[start : start + head]
+
+    def inverse_of(u):
+        return lax.rsqrt(jnp.mean(u * u, axis=0, keepdims=True) + 1e-06)
+
+    query_gain, key_gain = query_gain_ref[...], key_gain_ref[...]
+
+    def query_of(h):
+        u = raw(0, h)
+        inverse = inverse_of(u)
+        return u, inverse, (u * inverse * query_gain).astype(jnp.bfloat16)
+
+    def key_of(h):
+        u = raw(1, h)
+        inverse = inverse_of(u)
+        return u, inverse, (u * inverse * key_gain).astype(jnp.bfloat16)
+
+    for h in range(heads):
+        query, key = query_of(h)[2], key_of(h)[2]
+        value = raw(2, h).astype(jnp.bfloat16)
+        weights = jnp.where(same, jnp.exp(mm(key, query, (0, 0)) * scale), 0.0)
+        probs = weights / jnp.sum(weights, axis=0, keepdims=True)
+        keep[h] = probs
+        att[h * head : (h + 1) * head] = mm(value, probs.astype(jnp.bfloat16)).astype(jnp.bfloat16)
+
+    low_out = mm(att[...], out_down_ref[...], (0, 0)).astype(jnp.bfloat16)
+    low_vel = ADAPTER_SCALE * mm(low_out, out_up_ref[...])
+    for copy in out_copies:
+        copy.wait()
+    velocity = mm(out[...], att[...]).T + low_vel
+    step_size = 1.0 / SCHED
+    for s in range(steps):
+        span = slice(s * tokens, (s + 1) * tokens)
+        coupling, rest, inverse, advantage, factor = (coef_ref[s, i] for i in range(5))
+        state = before_ref[span].astype(jnp.float32)
+        vel = velocity[span]
+        mean_now = state - step_size * (vel + coupling * (state + rest * vel))
+        residual = after_ref[span].astype(jnp.float32) - mean_now
+        drift = mean_now - means_ref[span].astype(jnp.float32)
+        grad_mean = (BETA * drift - advantage * residual) * inverse
+        grad_vel[span] = (grad_mean * factor).astype(jnp.bfloat16)
+    gv = grad_vel[...]
+    out_up_grad = ADAPTER_SCALE * mm(low_out, gv, (0, 0))
+    grad_low = ADAPTER_SCALE * mm(gv, out_up_ref[...], (1, 1))
+    grad_low_t = grad_low.T.astype(jnp.bfloat16)
+    out_down_grad = mm(grad_low_t, att[...], (1, 1))
+    grad_att_rows = mm(gv, out[...]) + mm(
+        grad_low.astype(jnp.bfloat16), out_down_ref[...], (1, 1)
+    )
+    grad_att[...] = grad_att_rows.T.astype(jnp.bfloat16)
+
+    def back(u, inverse, gain, e):
+        scaled = e * gain
+        return inverse * scaled - u * (inverse * inverse * inverse) * jnp.mean(
+            scaled * u, axis=0, keepdims=True
+        )
+
+    for h in range(heads):
+        span = slice(h * head, (h + 1) * head)
+        query_raw, query_inverse, query = query_of(h)
+        key_raw, key_inverse, key = key_of(h)
+        value = raw(2, h).astype(jnp.bfloat16)
+        probs = keep[h]
+        upstream = grad_att[span]
+        grad_probs = mm(value, upstream, (0, 0))
+        delta = jnp.sum(
+            upstream.astype(jnp.float32) * att[span].astype(jnp.float32), axis=0, keepdims=True
+        )
+        grad_scores = (probs * (grad_probs - delta) * scale).astype(jnp.bfloat16)
+        grad_query = mm(key, grad_scores)
+        grad_key = mm(query, grad_scores, (1, 1)).astype(jnp.bfloat16).astype(jnp.float32)
+        grad_value = mm(upstream, probs.astype(jnp.bfloat16), (1, 1)).astype(jnp.bfloat16)
+        first, second, third = (i * inner + h * head for i in range(3))
+        grad_proj[first : first + head] = back(
+            query_raw, query_inverse, query_gain, grad_query
+        ).astype(jnp.bfloat16)
+        grad_proj[second : second + head] = back(
+            key_raw, key_inverse, key_gain, grad_key
+        ).astype(jnp.bfloat16)
+        grad_proj[third : third + head] = grad_value
+
+    up_grad = ADAPTER_SCALE * mm(low_t, grad_proj[...], (1, 1))
+    grad_low_qkv = (ADAPTER_SCALE * mm(up_ref[...], grad_proj[...])).astype(jnp.bfloat16)
+    down_grad = mm(grad_low_qkv, inputs[...])
+    at = 0
+    for grad in (down_grad, up_grad, out_down_grad, out_up_grad):
+        width = grad.shape[1] // members
+        for g in range(members):
+            parts_ref[g, :, at : at + width] = grad[:, g * width : (g + 1) * width].astype(
+                jnp.bfloat16
+            )
+        at += width
+
+
+def block_gradients(steps, coef, full, *rest):
+    before, query_gain, out_down, out_up = rest[0], rest[4], rest[8], rest[9]
+    up = rest[7]
+    members = full.shape[0]
+    rows, width = before.shape
+    inner, rank = out_down.shape
+    heads = inner // query_gain.shape[0]
+    share = (2 * width + 4 * inner) // members
+    bf, f32, dma = jnp.bfloat16, jnp.float32, pltpu.SemaphoreType.DMA
+    vmem = pl.BlockSpec(memory_space=pltpu.VMEM)
+    smem = pl.BlockSpec(memory_space=pltpu.SMEM)
+    return pl.pallas_call(
+        block_kernel,
+        out_shape=jax.ShapeDtypeStruct((members, rank, share), bf),
+        in_specs=[smem, smem, pl.BlockSpec(memory_space=pl.ANY)] + [vmem] * len(rest),
+        out_specs=vmem,
+        scratch_shapes=[
+            pltpu.VMEM((3 * inner, width), bf),
+            pltpu.VMEM((width, inner), bf),
+            pltpu.VMEM((rows, width), bf),
+            pltpu.VMEM((3 * inner, rows), f32),
+            pltpu.VMEM((heads, rows, rows), f32),
+            pltpu.VMEM((inner, rows), bf),
+            pltpu.VMEM((inner, rows), bf),
+            pltpu.VMEM((3 * inner, rows), bf),
+            pltpu.VMEM((rows, width), bf),
+            dma((members,)),
+            dma((2 * members,)),
+        ],
+        compiler_params=pltpu.CompilerParams(vmem_limit_bytes=48 * 1024 * 1024),
+        name="block_gradients",
+    )(steps, coef, full, *rest)
+
+
+def split_share(share, widths):
+    first, second, third = widths[0], widths[0] + widths[1], sum(widths[:3])
+    return (
+        share[:, :first].T,
+        share[:, first:second],
+        share[:, second:third].T,
+        share[:, third:],
     )
 
 
@@ -334,7 +560,7 @@
     sample_number = lax.axis_size("prm") * grp_count * steps_here
     member = (sample_prompt_index[0, 0] == jnp.arange(2, dtype=jnp.int32)).astype(jnp.float32)
     reward = rewards[0, 0]
-    direct = direct_fits(projection_weight, output_weight)
+    direct = direct_fits(projection_weight, output_weight, row_count)
     if direct:
         half = output_weight.shape[1] // 2
         qkv_own = projection_weight.shape[1]
@@ -348,19 +574,43 @@
         )
         full, notes = gather_weights(own, note)
         totals = jnp.sum(notes[:, :2, 0], axis=0)
-        full_qkv = full[:, :qkv_own].reshape(-1, model_width)
-        full_out = (
-            full[:, qkv_own:]
-            .reshape(grp_count, half, 2, inner_width)
-            .transpose(0, 2, 1, 3)
-            .reshape(model_width, inner_width)
-        )
-    else:
-        totals = lax.psum(member * reward, "grp")
-        full_qkv, full_out = (
-            lax.all_gather(projection_weight.T, "grp", axis=0, tiled=True),
-            lax.all_gather(output_weight.T, "grp", axis=0, tiled=True),
-        )
+        advantage = reward - jnp.sum(member * totals) / (grp_count // 2)
+        timestep_values = stored_step_index[0, 0]
+        time_now = 1.0 - timestep_values.astype(jnp.float32) / SCHED
+        variance = ETA * ETA * time_now / (1.0 - time_now) / SCHED
+        coupling = ETA * ETA / (2.0 * (1.0 - time_now))
+        coef = jnp.stack(
+            [
+                coupling,
+                1.0 - time_now,
+                1.0 / (sample_number * variance),
+                jnp.broadcast_to(advantage, coupling.shape),
+                -step_size * (1.0 + coupling * (1.0 - time_now)),
+            ],
+            axis=1,
+        )
+        parts = block_gradients(
+            timestep_values,
+            coef,
+            full,
+            latent_before_step.reshape(row_count, model_width),
+            latent_after_step.reshape(row_count, model_width),
+            reference_step_means.reshape(row_count, model_width),
+            modulation,
+            query_norm_gain[:, None],
+            key_norm_gain[:, None],
+            projection_down_weight,
+            projection_up_weight,
+            output_down_weight,
+            output_up_weight,
+        )
+        widths = [size // grp_count for size in (model_width, 3 * inner_width, inner_width)]
+        return split_share(reduce_shares(parts), widths)
+    totals = lax.psum(member * reward, "grp")
+    full_qkv, full_out = (
+        lax.all_gather(projection_weight.T, "grp", axis=0, tiled=True),
+        lax.all_gather(output_weight.T, "grp", axis=0, tiled=True),
+    )
     advantage_values = reward - jnp.sum(member * totals) / (grp_count // 2)
     timestep_values = stored_step_index[0, 0]
     time_now = 1.0 - timestep_values.astype(jnp.float32) / SCHED
@@ -511,20 +761,9 @@
         ],
         axis=2,
     )
-    if direct:
-        share = reduce_shares(packed.transpose(1, 0, 2))
-    else:
-        share = lax.psum_scatter(
-            packed, "grp", scatter_dimension=1, tiled=True
-        ).astype(jnp.float32).reshape(rank, -1)
-        share = lax.psum(share, ("seq", "prm"))
-    first, second, third = widths[0], widths[0] + widths[1], sum(widths[:3])
-    return (
-        share[:, :first].T,
-        share[:, first:second],
-        share[:, second:third].T,
-        share[:, third:],
-    )
+    share = lax.psum_scatter(packed, "grp", scatter_dimension=1, tiled=True)
+    share = lax.psum(share.astype(jnp.float32).reshape(rank, -1), ("seq", "prm"))
+    return split_share(share, widths)
 
 
 def solution(mesh):

time: 147 us -> 99.2 us (0.67)
  local copies, waits for them, and re-layouts: 39.8 us -> 7.66 us
  matrix products: 18.9 us -> 0 us
  Pallas kernels: 67.9 us -> 84.7 us
  other arithmetic: 15.5 us -> 3.58 us
    dot_general x18 -> x0, matrix products: 18.5 us -> none  [the longest x1 3.09 us: per_device(): jnp.einsum('shqk,shdk->shqd', grad_scores, key_cols, preferred_element_ty...]
    pallas_call x0 -> x1, Pallas kernels: none -> 16.8 us  [block_gradients(): pl.pallas_call(block_kernel, out_shape=jax.ShapeDtypeStruct((members, ran...]
    slice x6 -> x2, local copies, waits for them, and re-layouts: 11.5 us -> 2.91 us  [the longest x1 1.49 us: split_share(): share[:, first:second]]
    mul x6 -> x1, local copies, waits for them, and re-layouts: 7.62 us -> 0.09 us  [per_device(): variance = ETA * ETA * time_now / (1.0 - time_now) / SCHED]
    reshape x13 -> x0, local copies, waits for them, and re-layouts: 6.72 us -> none  [the longest x2 3.26 us: per_device(): attended_gradient.astype(jnp.bfloat16)]
    unnamed x72 -> x26, local copies, waits for them, and re-layouts: 6.11 us -> 1.21 us
    another operation x3 -> x0, other arithmetic: 3.79 us -> none  [per_device(): jnp.stack([grad_q_raw, grad_k_raw, grad_value], axis=2).astype(jnp.bfloat16)]
    reduce_sum x5 -> x1, other arithmetic: 3.25 us -> 0.6 us  [per_device(): advantage = reward - jnp.sum(member * totals) / (grp_count // 2)]
where the time goes in v2:
time: 99.2 us; the launch traced here: 98.8 us
  Pallas kernels  84.7 us (85%)
  local copies, waits for them, and re-layouts  7.66 us (8%)
  other arithmetic  3.58 us (4%)
  between operations  2.82 us (3%)
    pallas_call x1, Pallas kernels, gather_weights(): pl.pallas_call(gather_kernel, out_shape=(jax.ShapeDtypeStruct((members,)...  52.9 us
    pallas_call x1, Pallas kernels, block_gradients(): pl.pallas_call(block_kernel, out_shape=jax.ShapeDtypeStruct((members, ran...  16.8 us
    pallas_call x1, Pallas kernels, reduce_shares(): pl.pallas_call(reduce_kernel, out_shape=jax.ShapeDtypeStruct(share, jnp.f...  15.1 us

profile of v2, /device:TPU:0, one launch (start us, length us, event | category | flops | bytes accessed | tf_op | source)
XLA Modules:
  0.0 98.8 jit_solution(11710153235813024615)
XLA Ops:
  0.6 0.0 copy-start.7
  0.6 0.0 copy-start.8
  0.7 1.0 fusion.1
  1.6 0.0 copy-start.9
  1.6 0.0 copy-start.10
  1.6 0.0 copy-start.11
  1.7 0.0 copy-start.1
  1.7 0.0 copy-start.2
  1.7 0.0 copy-start.3
  1.7 0.0 copy-start.4
  1.7 0.0 copy-start.5
  1.7 0.0 copy-start.6
  1.7 2.0 %maximum_maximum_fusion.own_ref = bf16[192,1536]{1,0:T(8,128)(2,1)} fusion(bf16[48,768]{1,0:T(8,128)(2,1)S(1)} %get-tuple-element.11, bf16[48,768]{1,0:T(8,128)(2,1)S(1)} %get-tuple-element.10, bf16[144,1536]{1,0:T(8,128)(2,1)} %bitcast.26), kind=kLoop, calls=%fused_computation | loop fusion | flops 1769472 | bytes 1179648 | tf_op jit(solution)/shard_map/concatenate | solution.py:568
  5.0 0.7 broadcast_in_dim.12.note_ref
  5.7 52.9 %gather_weights.1 = (bf16[16,192,1536]{2,1,0:T(8,128)(2,1)}, f32[16,8,128]{2,1,0:T(8,128)}) custom-call(bf16[192,1536]{1,0:T(8,128)(2,1)} %maximum_maximum_fusion.own_ref, f32[8,128]{1,0:T(8,128)} %broadcast_in_dim.12.note_ref), custom_call_target="tpu_custom_call" | custom-call | tf_op jit(solution)/shard_map/gather_weights/pallas_call | solution.py:202
  58.6 1.0 slice_reduce_fusion
  59.5 0.6 fusion
  60.8 0.0 copy-done.7
  60.8 0.1 copy.19
  60.9 0.1 copy.20
  61.0 0.1 stack.2.coef_ref
  61.1 0.0 copy-done.8
  61.1 0.2 copy.26.down_ref
  61.4 0.0 copy-done.9
  61.4 0.2 copy.27.out_down_ref
  61.6 0.0 copy-done.10
  61.6 0.1 copy.24.query_gain_ref
  61.7 0.0 copy-done.11
  61.7 0.1 copy.25.key_gain_ref
  61.8 0.0 copy-done.1
  61.8 0.0 copy-done.2
  61.8 0.0 copy-done.3
  61.8 0.0 copy-done.4
  61.8 0.0 copy-done.5
  61.8 0.0 copy-done.6
  61.8 16.8 %block_gradients.1.parts_ref = bf16[16,32,384]{2,1,0:T(8,128)(2,1)S(1)} custom-call(s32[2]{0:T(128)S(1)} %bitcast.25, f32[2,5]{1,0:T(2,128)S(1)} %stack.2.coef_ref, bf16[16,192,1536]{2,1,0:T(8,128)(2,1)} %get-tuple-element.7.full_ref, bf16[128,1536]{1,0:T(8,128)(2,1)S(1)} %bitcast.22, bf16[128,1536]{1,0:T(8,128)(2,1)S(1)} %bitcast.23, ...), custom_call_target="tpu_custom_call" | custom-call | tf_op jit(solution)/shard_map/block_gradients/pallas_call | solution.py:500
  78.6 0.0 copy-start
  78.6 0.7 copy-done
  79.3 15.1 %reduce_shares.1 = f32[32,384]{1,0:T(8,128)} custom-call(bf16[16,32,384]{2,1,0:T(8,128)(2,1)} %copy-done), custom_call_target="tpu_custom_call" | custom-call | tf_op jit(solution)/shard_map/reduce_shares/pallas_call | solution.py:278
  94.4 1.4 %fusion.2 = (f32[32,96]{1,0:T(8,128)}, f32[96,32]{0,1:T(8,128)}) fusion(f32[32,384]{1,0:T(8,128)} %reduce_shares.1), kind=kLoop, calls=%fused_computation.14 | loop fusion | bytes 49152 | tf_op jit(solution)/shard_map/slice | solution.py:529
  95.8 1.5 %slice.25 = f32[32,144]{1,0:T(8,128)} slice(f32[32,384]{1,0:T(8,128)} %reduce_shares.1), slice={[0:32], [96:240]} | slice | bytes 36864 | tf_op jit(solution)/shard_map/slice | solution.py:527
  97.3 1.4 %slice_bitcast_fusion = f32[48,32]{0,1:T(8,128)} fusion(f32[32,384]{1,0:T(8,128)} %reduce_shares.1), kind=kLoop, calls=%fused_computation.1 | loop fusion | bytes 12288 | tf_op jit(solution)/shard_map/transpose | solution.py:528
  (5 shorter events, 0.0 us)
Async XLA Ops:
  0.6 60.2 %copy-start.7 = (s32[1,1,2]{2,1,0:T(1,128)S(1)}, s32[1,1,2]{2,1,0:T(1,128)}, u32[]{:S(2)}) copy-start(s32[1,1,2]{2,1,0:T(1,128)} %param.20) | copy-start | bytes 28
  0.6 60.5 %copy-start.8 = (bf16[1536,32]{0,1:T(8,128)(2,1)S(1)}, bf16[1536,32]{0,1:T(8,128)(2,1)}, u32[]{:S(2)}) copy-start(bf16[1536,32]{0,1:T(8,128)(2,1)} %param.26) | copy-start | bytes 294916
  1.6 59.7 %copy-start.9 = (bf16[768,32]{0,1:T(8,128)(2,1)S(1)}, bf16[768,32]{0,1:T(8,128)(2,1)}, u32[]{:S(2)}) copy-start(bf16[768,32]{0,1:T(8,128)(2,1)} %param.28) | copy-start | bytes 147460
  1.6 59.9 %copy-start.10 = (f32[64]{0:T(128)S(1)}, f32[64]{0:T(128)}, u32[]{:S(2)}) copy-start(f32[64]{0:T(128)} %param.24) | copy-start | bytes 772
  1.6 60.0 %copy-start.11 = (f32[64]{0:T(128)S(1)}, f32[64]{0:T(128)}, u32[]{:S(2)}) copy-start(f32[64]{0:T(128)} %param.25) | copy-start | bytes 772
  1.7 60.1 %copy-start.1 = (bf16[1,1,2,64,1536]{4,3,2,1,0:T(8,128)(2,1)S(1)}, bf16[1,1,2,64,1536]{4,3,2,1,0:T(8,128)(2,1)}, u32[]{:S(2)}) copy-start(bf16[1,1,2,64,1536]{4,3,2,1,0:T(8,128)(2,1)} %param.15) | copy-start | bytes 1179652
  1.7 60.1 %copy-start.2 = (bf16[1,1,2,64,1536]{4,3,2,1,0:T(8,128)(2,1)S(1)}, bf16[1,1,2,64,1536]{4,3,2,1,0:T(8,128)(2,1)}, u32[]{:S(2)}) copy-start(bf16[1,1,2,64,1536]{4,3,2,1,0:T(8,128)(2,1)} %param.16) | copy-start | bytes 1179652
  1.7 60.1 %copy-start.3 = (bf16[1,1,2,64,1536]{4,3,2,1,0:T(8,128)(2,1)S(1)}, bf16[1,1,2,64,1536]{4,3,2,1,0:T(8,128)(2,1)}, u32[]{:S(2)}) copy-start(bf16[1,1,2,64,1536]{4,3,2,1,0:T(8,128)(2,1)} %param.17) | copy-start | bytes 1179652
  1.7 60.1 %copy-start.4 = (bf16[32,2304]{1,0:T(8,128)(2,1)S(1)}, bf16[32,2304]{1,0:T(8,128)(2,1)}, u32[]{:S(2)}) copy-start(bf16[32,2304]{1,0:T(8,128)(2,1)} %up_ref.1) | copy-start | bytes 442372
  1.7 60.1 %copy-start.5 = (f32[10,2,1536]{2,1,0:T(2,128)S(1)}, f32[10,2,1536]{2,1,0:T(2,128)}, u32[]{:S(2)}) copy-start(f32[10,2,1536]{2,1,0:T(2,128)} %modulation_ref.1) | copy-start | bytes 368644
  1.7 60.1 %copy-start.6 = (bf16[32,1536]{1,0:T(8,128)(2,1)S(1)}, bf16[32,1536]{1,0:T(8,128)(2,1)}, u32[]{:S(2)}) copy-start(bf16[32,1536]{1,0:T(8,128)(2,1)} %out_up_ref.1) | copy-start | bytes 294916
  78.6 0.7 copy-start
